TPU v7x, 256 devices: a whole 4x4x8 slice. The times are simulated.
256 devices in a mesh: gx: 16 (over z, core), gy: 16 (over y, x).
Axes of the slice: x: 4, y: 4, z: 8, core: 2. Of those that a mesh axis runs over, the one named last changes fastest.
Arguments:
- modes: float32 [524288, 512], P(('gx', 'gy'))
- batch: float32 [524288, 256], P(('gx', 'gy')), as said below
- core: float32 [768, 512], replicated, may hold values from -0.21875 to 0.21875
Outputs:
- new_modes: float32 [524288, 512], P(('gx', 'gy'))
Inputs may be any that keep to these rules, and one draw needn't show every extreme that they name: Each row of modes and batch shares one positive scale; batch holds a sizeable part of the span of modes.
All inputs are finite; a program needn't handle non-finite values.
Results may differ from a plain program's by a relative error of at most 0.000058.
Values sent between devices are 32-bit elements; how exact they have to be, the bound alone decides.
A program may use at most 64 MiB of HBM per device.

v0:
```python
import jax
import jax.numpy as jnp
from jax import lax
from jax.sharding import PartitionSpec as P


def matmul(left, right):
    return jnp.dot(left, right, precision=lax.Precision.HIGHEST, preferred_element_type=jnp.float32)


def global_sum(parts):
    return lax.psum((parts[0],), ("gx", "gy"))


def shards(modes, batch, core):
    total_rows = modes.shape[0] * lax.axis_size("gx") * lax.axis_size("gy")
    width = modes.shape[1]
    top = matmul(modes, core[:width])
    cross = global_sum((matmul(modes.T, batch),))[0]
    coeffs = cross / total_rows
    resid = batch - matmul(modes, coeffs)
    gram = global_sum((matmul(resid.T, resid),))[0] / total_rows
    lower = jnp.linalg.cholesky(gram)
    basis = jax.scipy.linalg.solve_triangular(lower, resid.T, lower=True).T
    return top + matmul(basis, core[width:])


def solution(mesh):
    placed = (P(("gx", "gy"), None), P(("gx", "gy"), None), P())
    return jax.shard_map(
        shards, mesh=mesh, in_specs=placed, out_specs=P(("gx", "gy"), None), check_vma=False
    )
```

profile of v0, /device:TPU:2, one launch (start us, length us, event | category | flops | bytes accessed | tf_op | source)
XLA Modules:
  0.0 619.7 jit_solution(16031329301337902461)
XLA Ops:
  6.5 10.5 %fusion.20 = f32[512,256]{1,0:T(8,128)} fusion(f32[2048,512]{1,0:T(8,128)} %param.3, f32[2048,256]{1,0:T(8,128)} %param.4), kind=kOutput, calls=%fused_computation.42 | convolution fusion | flops 3221225472 | bytes 6815744 | tf_op jit(solution)/shard_map/dot_general | solution.py:8
  17.0 0.0 all-reduce.4.cloned.1.call-update
  17.0 0.5 all-reduce.6.cloned.1.call-start
  17.6 1.8 copy.4
  19.4 256.1 %all-reduce.4.cloned.1.call-done = f32[512,256]{1,0:T(8,128)} async-done(((f32[512,256]{1,0:T(8,128)}), f32[512,256]{1,0:T(8,128)}) %all-reduce.4.cloned.1.call-update) | async-done | bytes 524304 | tf_op jit(solution)/shard_map/psum | solution.py:12
  275.5 9.9 %fusion = f32[2048,256]{0,1:T(8,128)S(1)} fusion(f32[2048,256]{0,1:T(8,128)} %copy.4, f32[2048,512]{1,0:T(8,128)} %param.3, f32[512,256]{1,0:T(8,128)} %all-reduce.4.cloned.1.call-done), kind=kOutput, calls=%fused_computation.4 | convolution fusion | flops 3221880832 | bytes 8912896 | tf_op jit(solution)/shard_map/dot_general | solution.py:8
  285.5 2.6 fusion.21
  288.0 0.0 all-reduce.6.cloned.1.call-update
  288.1 10.2 %fusion.6 = f32[2048,512]{1,0:T(8,128)} fusion(f32[2048,512]{1,0:T(8,128)} %param.3, f32[768,512]{1,0:T(8,128)} %param.5), kind=kOutput, calls=%fused_computation.12 | convolution fusion | flops 6442450944 | bytes 9437184 | tf_op jit(solution)/shard_map/dot_general | solution.py:8
  298.3 242.9 %all-reduce.6.cloned.1.call-done = f32[256,256]{0,1:T(8,128)} async-done(((f32[256,256]{0,1:T(8,128)}), f32[256,256]{0,1:T(8,128)}) %all-reduce.6.cloned.1.call-update) | async-done | bytes 262160 | tf_op jit(solution)/shard_map/psum | solution.py:12
  541.2 1.0 broadcast_multiply_fusion
  542.2 0.1 copy.6
  542.3 1.0 fusion.10
  543.3 11.7 %cholesky.50 = f32[128,128]{1,0:T(8,128)S(1)} custom-call(f32[128,128]{1,0:T(8,128)S(1)} %cholesky.118), custom_call_target="Cholesky" | custom-call | tf_op jit(solution)/shard_map/jit(cholesky)/cholesky | solution.py:23
  555.0 9.8 %custom-call.15 = f32[1,128,128]{1,2,0:T(8,128)S(1)} custom-call(f32[1,128,128]{2,1,0:T(8,128)S(1)} %get-tuple-element.26), custom_call_target="InvertDiagBlocksLowerTriangular" | custom-call | tf_op jit(solution)/shard_map/jit(cholesky)/cholesky | solution.py:23
  564.9 0.2 constant_dynamic-update-slice_fusion.1
  565.1 0.3 convolution_subtract_fusion.1
  565.4 11.7 %cholesky.105 = f32[128,128]{1,0:T(8,128)S(1)} custom-call(f32[128,128]{1,0:T(8,128)S(1)} %convolution_subtract_fusion.1), custom_call_target="Cholesky" | custom-call | tf_op jit(solution)/shard_map/jit(cholesky)/cholesky | solution.py:23
  577.1 0.7 compare_reduce_fusion
  579.1 0.1 triangular_solve.57
  579.2 4.1 while.1
  579.2 0.7 fusion.33
  579.9 1.3 bitcast_dynamic-update-slice_fusion.2
  581.2 0.7 fusion.33
  581.9 1.3 bitcast_dynamic-update-slice_fusion.2
  583.3 19.9 %custom-call.16 = f32[2,128,128]{1,2,0:T(8,128)S(1)} custom-call(f32[2,128,128]{2,1,0:T(8,128)S(1)} %get-tuple-element.12), custom_call_target="InvertDiagBlocksLowerTriangular" | custom-call | tf_op jit(solution)/shard_map/jit(_solve_triangular)/triangular_solve | solution.py:24
  603.2 1.1 fusion.4
  604.2 0.0 copy-start
  604.2 1.0 convolution_subtract_fusion
  605.2 1.1 fusion.13
  606.3 0.1 copy-done
  606.4 6.2 %convolution_add_fusion = f32[2048,512]{1,0:T(8,128)} fusion(f32[2048,512]{1,0:T(8,128)S(1)} %copy-done, f32[128,2048]{1,0:T(8,128)S(1)} %fusion.13, f32[128,2048]{1,0:T(8,128)S(1)} %fusion.4, f32[768,512]{1,0:T(8,128)} %param.5), kind=kOutput, calls=%fused_computation.2 | convolution fusion | flops 3222798336 | bytes 11010048 | tf_op jit(solution)/shard_map/dot_general | solution.py:8
  (12 shorter events, 0.2 us)
Async XLA Ops:
  6.5 11.0 %copy-start.1 = (f32[2048,256]{1,0:T(8,128)S(1)}, f32[2048,256]{1,0:T(8,128)}, u32[]{:S(2)}) copy-start(f32[2048,256]{1,0:T(8,128)} %param.4) | copy-start | bytes 6291460
  6.5 269.0 %all-reduce.4.cloned.1.call-start = ((), (), s32[]{:S(2)}) async-start(), calls=%async_computation | async-start | bytes 1048576 | tf_op jit(solution)/shard_map/psum | solution.py:12
  17.0 524.1 %all-reduce.6.cloned.1.call-start = ((), (), s32[]{:S(2)}) async-start(), calls=%async_computation.1 | async-start | bytes 524288 | tf_op jit(solution)/shard_map/psum | solution.py:12
  604.2 2.2 copy-start
Sparse Core Ops, SparseCore 0:
  17.2 258.3 all-reduce.3
  288.2 252.9 all-reduce.5
where the time goes:
time: 625 us; the launch traced here: 620 us
  waiting for transfers between devices  499 us (80%)
  other arithmetic  55.9 us (9%)
  matrix products  43 us (7%)
  between operations  15 us (2%)
    psum x2, waiting for transfers between devices, global_sum(): return lax.psum((parts[0],), ('gx', 'gy'))  499 us
    dot_general x5, matrix products, matmul(): jnp.dot(left, right, precision=lax.Precision.HIGHEST, preferred_element_t...  39.5 us
    another operation x6, other arithmetic, shards(): lower = jnp.linalg.cholesky(gram)  34 us
    another operation x3, other arithmetic, shards(): basis = jax.scipy.linalg.solve_triangular(lower, resid.T, lower=True).T  19.9 us
  transfers between devices with their start and end apart: 2, of which 2 were waited for; matrix products, arithmetic and copies ran while one was open for 2% of the time, Pallas kernels for 0%

commit v1 on v0

--- a/solution.py
+++ b/solution.py
@@ -9,7 +9,7 @@
 
 
 def global_sum(parts):
-    return lax.psum((parts[0],), ("gx", "gy"))
+    return lax.psum(lax.psum((parts[0],), "gx"), "gy")
 
 
 def shards(modes, batch, core):

time: 625 us -> 534 us (0.85)
  waiting for transfers between devices: 499 us -> 408 us
    psum x2 -> x4, waiting for transfers between devices: 499 us -> 408 us  [global_sum(): return lax.psum(lax.psum((parts[0],), 'gx'), 'gy')]
  transfers between devices with their start and end apart: 2 -> 4, of which waited for: 2 -> 4; matrix products, arithmetic and copies ran while one was open for 2% -> 2% of each run, Pallas kernels for 0% -> 0%
where the time goes in v1:
time: 534 us; the launch traced here: 529 us
  waiting for transfers between devices  408 us (76%)
  other arithmetic  55.9 us (10%)
  matrix products  43 us (8%)
  between operations  14.8 us (3%)
  local copies, waits for them, and re-layouts  6.17 us (1%)
    psum x4, waiting for transfers between devices, global_sum(): return lax.psum(lax.psum((parts[0],), 'gx'), 'gy')  408 us
    dot_general x5, matrix products, matmul(): jnp.dot(left, right, precision=lax.Precision.HIGHEST, preferred_element_t...  39.4 us
    another operation x6, other arithmetic, shards(): lower = jnp.linalg.cholesky(gram)  34 us
    another operation x3, other arithmetic, shards(): basis = jax.scipy.linalg.solve_triangular(lower, resid.T, lower=True).T  19.9 us
  transfers between devices with their start and end apart: 4, of which 4 were waited for; matrix products, arithmetic and copies ran while one was open for 2% of the time, Pallas kernels for 0%

profile of v1, /device:TPU:2, one launch (start us, length us, event | category | flops | bytes accessed | tf_op | source)
XLA Modules:
  0.0 528.9 jit_solution(4050120570851998627)
XLA Ops:
  6.5 10.5 %fusion.20 = f32[512,256]{1,0:T(8,128)} fusion(f32[2048,512]{1,0:T(8,128)} %param.3, f32[2048,256]{1,0:T(8,128)} %param.4), kind=kOutput, calls=%fused_computation.42 | convolution fusion | flops 3221225472 | bytes 6815744 | tf_op jit(solution)/shard_map/dot_general | solution.py:8
  17.1 113.8 %all-reduce.6.cloned.1.call-done = f32[512,256]{1,0:T(8,128)} async-done(((f32[512,256]{1,0:T(8,128)}), f32[512,256]{1,0:T(8,128)}) %all-reduce.6.cloned.1.call-update) | async-done | bytes 524304 | tf_op jit(solution)/shard_map/psum | solution.py:12
  130.9 0.5 all-reduce.10.cloned.1.call-start
  131.4 1.8 copy.4
  133.2 96.8 %all-reduce.8.cloned.1.call-done = f32[512,256]{1,0:T(8,128)} async-done(((f32[512,256]{1,0:T(8,128)}), f32[512,256]{1,0:T(8,128)}) %all-reduce.8.cloned.1.call-update) | async-done | bytes 524304 | tf_op jit(solution)/shard_map/psum | solution.py:12
  230.0 9.9 %fusion = f32[2048,256]{0,1:T(8,128)S(1)} fusion(f32[2048,256]{0,1:T(8,128)} %copy.4, f32[2048,512]{1,0:T(8,128)} %param.3, f32[512,256]{1,0:T(8,128)} %all-reduce.8.cloned.1.call-done), kind=kOutput, calls=%fused_computation.4 | convolution fusion | flops 3221880832 | bytes 8912896 | tf_op jit(solution)/shard_map/dot_general | solution.py:8
  239.9 2.6 fusion.21
  242.5 0.0 all-reduce.12.cloned.1.call-start
  242.6 109.9 %all-reduce.10.cloned.1.call-done = f32[256,256]{0,1:T(8,128)} async-done(((f32[256,256]{0,1:T(8,128)}), f32[256,256]{0,1:T(8,128)}) %all-reduce.10.cloned.1.call-update) | async-done | bytes 262160 | tf_op jit(solution)/shard_map/psum | solution.py:12
  352.4 10.2 %fusion.6 = f32[2048,512]{1,0:T(8,128)} fusion(f32[2048,512]{1,0:T(8,128)} %param.3, f32[768,512]{1,0:T(8,128)} %param.5), kind=kOutput, calls=%fused_computation.12 | convolution fusion | flops 6442450944 | bytes 9437184 | tf_op jit(solution)/shard_map/dot_general | solution.py:8
  362.7 88.0 %all-reduce.12.cloned.1.call-done = f32[256,256]{0,1:T(8,128)} async-done(((f32[256,256]{0,1:T(8,128)}), f32[256,256]{0,1:T(8,128)}) %all-reduce.12.cloned.1.call-update) | async-done | bytes 262160 | tf_op jit(solution)/shard_map/psum | solution.py:12
  450.7 1.0 broadcast_multiply_fusion
  451.7 0.1 copy.6
  451.8 1.0 fusion.10
  452.8 11.7 %cholesky.50 = f32[128,128]{1,0:T(8,128)S(1)} custom-call(f32[128,128]{1,0:T(8,128)S(1)} %cholesky.118), custom_call_target="Cholesky" | custom-call | tf_op jit(solution)/shard_map/jit(cholesky)/cholesky | solution.py:23
  464.5 9.8 %custom-call.15 = f32[1,128,128]{1,2,0:T(8,128)S(1)} custom-call(f32[1,128,128]{2,1,0:T(8,128)S(1)} %get-tuple-element.26), custom_call_target="InvertDiagBlocksLowerTriangular" | custom-call | tf_op jit(solution)/shard_map/jit(cholesky)/cholesky | solution.py:23
  474.4 0.2 constant_dynamic-update-slice_fusion.1
  474.6 0.3 convolution_subtract_fusion.1
  474.9 11.7 %cholesky.105 = f32[128,128]{1,0:T(8,128)S(1)} custom-call(f32[128,128]{1,0:T(8,128)S(1)} %convolution_subtract_fusion.1), custom_call_target="Cholesky" | custom-call | tf_op jit(solution)/shard_map/jit(cholesky)/cholesky | solution.py:23
  486.6 0.7 compare_reduce_fusion
  488.6 0.1 triangular_solve.57
  488.7 4.1 while.1
  488.7 0.7 fusion.33
  489.4 1.3 bitcast_dynamic-update-slice_fusion.2
  490.7 0.7 fusion.33
  491.4 1.3 bitcast_dynamic-update-slice_fusion.2
  492.8 19.9 %custom-call.16 = f32[2,128,128]{1,2,0:T(8,128)S(1)} custom-call(f32[2,128,128]{2,1,0:T(8,128)S(1)} %get-tuple-element.12), custom_call_target="InvertDiagBlocksLowerTriangular" | custom-call | tf_op jit(solution)/shard_map/jit(_solve_triangular)/triangular_solve | solution.py:24
  512.7 1.1 fusion.4
  513.7 1.0 convolution_subtract_fusion
  514.8 1.1 fusion.13
  515.8 0.1 copy-done
  515.9 6.2 %convolution_add_fusion = f32[2048,512]{1,0:T(8,128)} fusion(f32[2048,512]{1,0:T(8,128)S(1)} %copy-done, f32[128,2048]{1,0:T(8,128)S(1)} %fusion.13, f32[128,2048]{1,0:T(8,128)S(1)} %fusion.4, f32[768,512]{1,0:T(8,128)} %param.5), kind=kOutput, calls=%fused_computation.2 | convolution fusion | flops 3222798336 | bytes 11010048 | tf_op jit(solution)/shard_map/dot_general | solution.py:8
  (18 shorter events, 0.3 us)
Async XLA Ops:
  6.5 124.3 %all-reduce.6.cloned.1.call-start = ((), (), s32[]{:S(2)}) async-start(), calls=%async_computation | async-start | bytes 1048576 | tf_op jit(solution)/shard_map/psum | solution.py:12
  6.5 124.9 %copy-start.1 = (f32[2048,256]{1,0:T(8,128)S(1)}, f32[2048,256]{1,0:T(8,128)}, u32[]{:S(2)}) copy-start(f32[2048,256]{1,0:T(8,128)} %param.4) | copy-start | bytes 6291460
  17.0 212.9 %all-reduce.8.cloned.1.call-start = ((), (), s32[]{:S(2)}) async-start(), calls=%async_computation.1 | async-start | bytes 1048576 | tf_op jit(solution)/shard_map/psum | solution.py:12
  130.9 221.5 %all-reduce.10.cloned.1.call-start = ((), (), s32[]{:S(2)}) async-start(), calls=%async_computation.2 | async-start | bytes 524288 | tf_op jit(solution)/shard_map/psum | solution.py:12
  242.5 208.2 %all-reduce.12.cloned.1.call-start = ((), (), s32[]{:S(2)}) async-start(), calls=%async_computation.3 | async-start | bytes 524288 | tf_op jit(solution)/shard_map/psum | solution.py:12
  513.7 2.2 copy-start
Sparse Core Ops, SparseCore 0:
  17.1 113.6 all-reduce.5
  134.1 95.8 all-reduce.7
  242.6 109.7 all-reduce.9
  355.4 95.2 all-reduce.11
